TPU v7x, 256 devices: a whole 4x4x8 slice. The times are simulated.
256 devices in a mesh: row: 16 (over x_lo, y, core), col: 16 (over x_hi, z).
Axes of the slice: x: 4 (x_hi: 2, x_lo: 2; x = x_hi * 2 + x_lo), y: 4, z: 8, core: 2. Of those that a mesh axis runs over, the one named last changes fastest.
Arguments:
- tokens: bfloat16 [512, 8192], P('col', 'row'), may hold values from -6 to 6
- cotangent: bfloat16 [512, 8192], P('col', 'row'), may hold values from -6 to 6
- gate_weight: bfloat16 [8192, 28672], P('row', 'col'), may hold values from -0.09375 to 0.09375
- up_weight: bfloat16 [8192, 28672], P('row', 'col'), may hold values from -0.09375 to 0.09375
- down_weight: bfloat16 [28672, 8192], P('col', 'row'), may hold values from -0.0625 to 0.0625
- gate_mask: int32 [64, 224], P('row', 'col'), may hold values 0 or 1
- up_mask: int32 [64, 224], P('row', 'col'), may hold values 0 or 1
- down_mask: int32 [224, 64], P('col', 'row'), may hold values 0 or 1
Outputs:
- output: bfloat16 [512, 8192], P('col', 'row')
- d_tokens: bfloat16 [512, 8192], P('col', 'row')
- grad_gate: bfloat16 [8192, 28672], P('row', 'col')
- grad_up: bfloat16 [8192, 28672], P('row', 'col')
- grad_down: bfloat16 [28672, 8192], P('col', 'row')
Inputs may be any that keep to these rules, and one draw needn't show every extreme that they name: `gate_mask`: 1 keeps a block, 0 prunes it. `up_mask`: 1 keeps a block, 0 prunes it. `down_mask`: 1 keeps a block, 0 prunes it.
All inputs are finite; a program needn't handle non-finite values.
Results may differ from a plain program's by a relative error of at most 0.0049.
Values may be sent and summed in bfloat16 or wider, within the bound.
No kernel may reach another device: no remote copies, remote signals or barrier semaphores. Data moves between devices by JAX's collectives and lax.ppermute only.
A program may use at most 128 MiB of HBM per device.

v0:
```python
import jax
import jax.numpy as jnp
from jax import lax
from jax.sharding import PartitionSpec as P


def masked(weight, block_mask):
    block_rows, block_cols = block_mask.shape
    total_rows, total_cols = weight.shape
    shaped = weight.reshape(
        block_rows, total_rows // block_rows, block_cols, total_cols // block_cols
    )
    return (shaped * block_mask.astype(weight.dtype)[:, None, :, None]).reshape(
        total_rows, total_cols
    )


def right_product(left, right):
    return lax.dot_general(
        left, right, (((1,), (1,)), ((), ())), preferred_element_type=jnp.float32
    )


def left_product(left, right):
    return lax.dot_general(
        left, right, (((0,), (0,)), ((), ())), preferred_element_type=jnp.float32
    )


def per_device(
    tokens, cotangent, gate_weight, up_weight, down_weight, gate_mask, up_mask, down_mask
):
    gate_eff = masked(gate_weight, gate_mask)
    up_eff = masked(up_weight, up_mask)
    down_eff = masked(down_weight, down_mask)
    rows_all, cot_all = (
        lax.all_gather(tokens, "col", axis=0, tiled=True),
        lax.all_gather(cotangent, "col", axis=0, tiled=True),
    )
    gate_part = jnp.dot(rows_all, gate_eff, preferred_element_type=jnp.float32)
    up_part = jnp.dot(rows_all, up_eff, preferred_element_type=jnp.float32)
    row_share = rows_all.shape[0] // lax.axis_size("row")
    gate_full, up_full = lax.psum((gate_part, up_part), "row")
    activated_full = gate_full * jax.nn.sigmoid(gate_full)
    hidden_all = (activated_full * up_full).astype(jnp.bfloat16)
    row_start = lax.axis_index("row") * row_share
    gate_share = lax.dynamic_slice_in_dim(gate_full, row_start, row_share, 0)
    up_share = lax.dynamic_slice_in_dim(up_full, row_start, row_share, 0)
    output = lax.psum_scatter(
        jnp.dot(hidden_all, down_eff, preferred_element_type=jnp.float32),
        "col",
        scatter_dimension=0,
        tiled=True,
    ).astype(jnp.bfloat16)
    hidden_part = right_product(cot_all, down_eff)
    hidden_grad = lax.psum_scatter(hidden_part, "row", scatter_dimension=0, tiled=True)
    sigmoid_gate = jax.nn.sigmoid(gate_share)
    activated = gate_share * sigmoid_gate
    gate_grad = (
        hidden_grad * up_share * sigmoid_gate * (1.0 + gate_share * (1.0 - sigmoid_gate))
    ).astype(jnp.bfloat16)
    up_grad = (hidden_grad * activated).astype(jnp.bfloat16)
    gate_grad_all, up_grad_all = (
        lax.all_gather(gate_grad, "row", axis=0, tiled=True),
        lax.all_gather(up_grad, "row", axis=0, tiled=True),
    )
    grad_down = masked(left_product(hidden_all, cot_all), down_mask).astype(jnp.bfloat16)
    grad_gate = masked(left_product(rows_all, gate_grad_all), gate_mask).astype(jnp.bfloat16)
    grad_up = masked(left_product(rows_all, up_grad_all), up_mask).astype(jnp.bfloat16)
    d_tokens = lax.psum_scatter(
        right_product(gate_grad_all, gate_eff) + right_product(up_grad_all, up_eff),
        "col",
        scatter_dimension=0,
        tiled=True,
    ).astype(jnp.bfloat16)
    return (output, d_tokens, grad_gate, grad_up, grad_down)


def solution(mesh):
    in_specs = (
        P("col", "row"),
        P("col", "row"),
        P("row", "col"),
        P("row", "col"),
        P("col", "row"),
        P("row", "col"),
        P("row", "col"),
        P("col", "row"),
    )
    out_specs = (
        P("col", "row"),
        P("col", "row"),
        P("row", "col"),
        P("row", "col"),
        P("col", "row"),
    )
    return jax.shard_map(
        per_device, mesh=mesh, in_specs=in_specs, out_specs=out_specs, check_vma=False
    )
```

profile of v0, /device:TPU:8, one launch (start us, length us, event | category | flops | bytes accessed | tf_op | source)
XLA Modules:
  0.0 772.1 jit_solution(7239612085857985313)
XLA Ops:
  7.2 47.2 %all_gather.12 = bf16[512,512]{1,0:T(8,128)(2,1)S(1)} all-gather(bf16[32,512]{1,0:T(8,128)(2,1)} %param.8), channel_id=1, replica_groups=mesh['row'=16,'col'=16] {'col'}, dimensions={0}, use_global_device_ids=true | all-gather | bytes 557056 | tf_op jit(solution)/shard_map/all_gather | solution.py:37
  54.4 0.8 fusion.6
  55.2 0.1 copy.44
  55.3 2.8 copy.45
  58.2 0.1 copy.41
  58.3 4.4 copy.42
  62.6 0.5 mul.97
  63.2 3.1 convolution_bitcast_fusion.1
  66.3 0.5 mul.93
  66.9 1.2 copy-done.4
  68.1 3.1 convolution_bitcast_fusion.2
  71.2 0.6 copy-done.12
  71.9 0.1 copy.47
  72.0 38.3 %all_gather.13 = bf16[512,512]{1,0:T(8,128)(2,1)S(1)} all-gather(bf16[32,512]{1,0:T(8,128)(2,1)S(1)} %copy-done.10), channel_id=1, replica_groups=mesh['row'=16,'col'=16] {'col'}, dimensions={0}, use_global_device_ids=true | all-gather | bytes 557056 | tf_op jit(solution)/shard_map/all_gather | solution.py:38
  110.3 0.5 mul.101
  110.8 4.6 convolution_bitcast_fusion
  115.4 5.2 copy.57
  120.6 0.0 all-gather.3.cloned.1.call-start
  120.7 86.0 %all-reduce.3.cloned.1.call-done = (f32[512,1792]{1,0:T(8,128)}, f32[512,1792]{1,0:T(8,128)}) async-done(((f32[512,1792]{1,0:T(8,128)}, f32[512,1792]{1,0:T(8,128)}), (f32[512,1792]{1,0:T(8,128)}, f32[512,1792]{1,0:T(8,128)})) %all-reduce.3.cloned.1.call-update) | async-done | bytes 7340048 | tf_op jit(solution)/shard_map/psum | solution.py:43
  206.7 71.8 %reduce-scatter.10.cloned.1.call-done = f32[32,1792]{1,0:T(8,128)} async-done(((f32[512,1792]{1,0:T(8,128)}), f32[32,1792]{1,0:T(8,128)}) %reduce-scatter.10.cloned.1.call-update) | async-done | bytes 229392 | tf_op jit(solution)/shard_map/reduce_scatter | solution.py:56
  278.5 2.0 multiply_convert_fusion.1
  280.5 0.5 all-gather.5.cloned.1.call-update
  281.1 4.3 multiply_convert_fusion
  285.4 1.3 copy-done.5
  286.7 2.1 fusion.4
  288.9 0.2 reduce-scatter.8.cloned.1.call-start
  289.1 29.6 %all-gather.3.cloned.1.call-done = bf16[512,1792]{1,0:T(8,128)(2,1)} async-done(((bf16[32,1792]{1,0:T(8,128)(2,1)}), bf16[512,1792]{1,0:T(8,128)(2,1)}) %all-gather.3.cloned.1.call-update) | async-done | bytes 1835024 | tf_op jit(solution)/shard_map/all_gather | solution.py:64
  318.7 4.7 fusion.3
  323.5 33.0 %all-gather.5.cloned.1.call-done = bf16[512,1792]{1,0:T(8,128)(2,1)} async-done(((bf16[32,1792]{1,0:T(8,128)(2,1)}), bf16[512,1792]{1,0:T(8,128)(2,1)}) %all-gather.5.cloned.1.call-update) | async-done | bytes 1835024 | tf_op jit(solution)/shard_map/all_gather | solution.py:65
  356.5 4.5 convolution_add_fusion
  360.9 0.1 copy.50
  361.0 0.1 copy.51
  361.1 0.1 copy.52
  361.2 0.5 mul.117
  361.8 1.0 copy-done.6
  362.7 2.4 fusion
  365.1 196.2 %reduce-scatter.6.cloned.1.call-done = f32[32,512]{1,0:T(8,128)} async-done(((f32[512,512]{1,0:T(8,128)}), f32[32,512]{1,0:T(8,128)}) %reduce-scatter.6.cloned.1.call-update) | async-done | bytes 65552 | tf_op jit(solution)/shard_map/reduce_scatter | solution.py:49
  561.3 1.5 convert_element_type.46
  562.8 0.5 mul.111
  563.3 1.0 copy-done.8
  564.3 1.2 fusion.2
  565.5 2.4 copy.53
  567.9 0.5 mul.114
  568.4 1.0 copy-done.9
  569.4 1.2 fusion.1
  570.5 2.4 copy.54
  572.9 190.9 %reduce-scatter.8.cloned.1.call-done = f32[32,512]{1,0:T(8,128)} async-done(((f32[512,512]{1,0:T(8,128)}), f32[32,512]{1,0:T(8,128)}) %reduce-scatter.8.cloned.1.call-update) | async-done | bytes 65552 | tf_op jit(solution)/shard_map/reduce_scatter | solution.py:70
  763.8 1.5 convert_element_type.49
  (31 shorter events, 0.3 us)
Async XLA Ops:
  7.2 199.5 %all-reduce.3.cloned.1.call-start = ((), (), s32[]{:S(2)}) async-start(), calls=%async_computation.8 | async-start | bytes 14680064 | tf_op jit(solution)/shard_map/psum | solution.py:43
  55.3 2.8 copy-start.11
  58.1 5.0 copy-start
  63.2 3.1 copy-start.2
  66.3 1.8 copy-start.3
  66.9 1.2 copy-start.4
  71.2 0.7 copy-start.12
  71.2 0.8 copy-start.10
  71.2 207.3 %reduce-scatter.10.cloned.1.call-start = ((), (), s32[]{:S(2)}) async-start(), calls=%async_computation.7 | async-start | bytes 3899392 | tf_op jit(solution)/shard_map/reduce_scatter | solution.py:56
  120.6 198.1 %all-gather.3.cloned.1.call-start = ((), (), s32[]{:S(2)}) async-start(), calls=%async_computation.4 | async-start | bytes 1949696 | tf_op jit(solution)/shard_map/all_gather | solution.py:64
  280.5 76.0 %all-gather.5.cloned.1.call-start = ((), (), s32[]{:S(2)}) async-start(), calls=%async_computation.5 | async-start | bytes 1949696 | tf_op jit(solution)/shard_map/all_gather | solution.py:65
  281.0 280.3 %reduce-scatter.6.cloned.1.call-start = ((), (), s32[]{:S(2)}) async-start(), calls=%async_computation.3 | async-start | bytes 1114112 | tf_op jit(solution)/shard_map/reduce_scatter | solution.py:49
  281.1 5.6 copy-start.7
  285.4 1.3 copy-start.5
  288.9 67.6 %copy-start.1 = (bf16[512,1792]{0,1:T(8,128)(2,1)S(1)}, bf16[512,1792]{0,1:T(8,128)(2,1)}, u32[]{:S(2)}) copy-start(bf16[512,1792]{0,1:T(8,128)(2,1)} %copy-done) | copy-start | bytes 5505028
  288.9 474.9 %reduce-scatter.8.cloned.1.call-start = ((), (), s32[]{:S(2)}) async-start(), calls=%async_computation.6 | async-start | bytes 1114112 | tf_op jit(solution)/shard_map/reduce_scatter | solution.py:70
  361.2 1.5 copy-start.6
  562.8 1.5 copy-start.8
  567.9 1.5 copy-start.9
Sparse Core Ops, SparseCore 0:
  71.3 135.3 all-reduce.2
  209.3 69.1 reduce-scatter.9
  280.6 38.1 all-gather.2
  320.4 35.9 all-gather.4
  360.1 201.1 reduce-scatter.5
  565.0 198.7 reduce-scatter.7
where the time goes:
time: 773 us; the launch traced here: 772 us
  waiting for transfers between devices  608 us (79%)
  blocking collectives  85.5 us (11%)
  local copies, waits for them, and re-layouts  27 us (3%)
  matrix products  26.8 us (3%)
  between operations  14.3 us (2%)
  other arithmetic  9.96 us (1%)
    reduce_scatter x1, waiting for transfers between devices, per_device(): lax.psum_scatter(jnp.dot(hidden_all, down_eff, preferred_element_type=jnp...  196 us
    reduce_scatter x1, waiting for transfers between devices, per_device(): lax.psum_scatter(right_product(gate_grad_all, gate_eff) + right_product(u...  191 us
    psum x1, waiting for transfers between devices, per_device(): gate_full, up_full = lax.psum((gate_part, up_part), 'row')  86 us
    reduce_scatter x1, waiting for transfers between devices, per_device(): lax.psum_scatter(hidden_part, 'row', scatter_dimension=0, tiled=True)  71.8 us
    all_gather x1, blocking collectives, per_device(): lax.all_gather(tokens, 'col', axis=0, tiled=True)  47.2 us
    all_gather x1, blocking collectives, per_device(): lax.all_gather(cotangent, 'col', axis=0, tiled=True)  38.3 us
    all_gather x1, waiting for transfers between devices, per_device(): lax.all_gather(up_grad, 'row', axis=0, tiled=True)  33 us
    all_gather x1, waiting for transfers between devices, per_device(): lax.all_gather(gate_grad, 'row', axis=0, tiled=True)  29.6 us
  transfers between devices with their start and end apart: 6, of which 6 were waited for; matrix products, arithmetic and copies ran while one was open for 5% of the time, Pallas kernels for 0%

commit v1 on v0

--- a/solution.py
+++ b/solution.py
@@ -61,7 +61,9 @@
     ).astype(jnp.bfloat16)
     up_grad = (hidden_grad * activated).astype(jnp.bfloat16)
     gate_grad_all, up_grad_all = (
-        lax.all_gather(gate_grad, "row", axis=0, tiled=True),
+        jnp.concatenate(
+            lax.all_to_all(jnp.stack([gate_grad] * lax.axis_size("row")), "row", 0, 0), axis=0
+        ),
         lax.all_gather(up_grad, "row", axis=0, tiled=True),
     )
     grad_down = masked(left_product(hidden_all, cot_all), down_mask).astype(jnp.bfloat16)

time: 773 us -> 747 us (0.966)
  waiting for transfers between devices: 608 us -> 572 us
  starting transfers between devices: 0.42 us -> 9.14 us
    all_gather x1 -> x0, waiting for transfers between devices: 29.6 us -> none  [per_device(): lax.all_gather(gate_grad, 'row', axis=0, tiled=True)]
    all_gather x1, waiting for transfers between devices: 33 us -> 9.75 us  [per_device(): lax.all_gather(up_grad, 'row', axis=0, tiled=True)]
    all_to_all x0 -> x1, waiting for transfers between devices: none -> 17.1 us  [per_device(): lax.all_to_all(jnp.stack([gate_grad] * lax.axis_size('row')), 'row', 0, 0)]
    all_to_all x0 -> x1, starting transfers between devices: none -> 8.76 us  [per_device(): lax.all_to_all(jnp.stack([gate_grad] * lax.axis_size('row')), 'row', 0, 0)]
    unnamed x31 -> x29, local copies, waits for them, and re-layouts: 23.2 us -> 22.2 us
  transfers between devices with their start and end apart: 6 -> 6, of which waited for: 6 -> 6; matrix products, arithmetic and copies ran while one was open for 5% -> 6% of each run, Pallas kernels for 0% -> 0%
where the time goes in v1:
time: 747 us; the launch traced here: 746 us
  waiting for transfers between devices  572 us (77%)
  blocking collectives  85.5 us (11%)
  matrix products  28.4 us (4%)
  local copies, waits for them, and re-layouts  27.4 us (4%)
  between operations  13.9 us (2%)
  other arithmetic  9.92 us (1%)
  starting transfers between devices  9.14 us (1%)
    reduce_scatter x1, waiting for transfers between devices, per_device(): lax.psum_scatter(right_product(gate_grad_all, gate_eff) + right_product(u...  196 us
    reduce_scatter x1, waiting for transfers between devices, per_device(): lax.psum_scatter(jnp.dot(hidden_all, down_eff, preferred_element_type=jnp...  191 us
    psum x1, waiting for transfers between devices, per_device(): gate_full, up_full = lax.psum((gate_part, up_part), 'row')  86.1 us
    reduce_scatter x1, waiting for transfers between devices, per_device(): lax.psum_scatter(hidden_part, 'row', scatter_dimension=0, tiled=True)  71.8 us
    all_gather x1, blocking collectives, per_device(): lax.all_gather(tokens, 'col', axis=0, tiled=True)  47.2 us
    all_gather x1, blocking collectives, per_device(): lax.all_gather(cotangent, 'col', axis=0, tiled=True)  38.3 us
    unnamed x29, local copies, waits for them, and re-layouts  22.2 us
    all_to_all x1, waiting for transfers between devices, per_device(): lax.all_to_all(jnp.stack([gate_grad] * lax.axis_size('row')), 'row', 0, 0)  17.1 us
  transfers between devices with their start and end apart: 6, of which 6 were waited for; matrix products, arithmetic and copies ran while one was open for 6% of the time, Pallas kernels for 0%

profile of v1, /device:TPU:8, one launch (start us, length us, event | category | flops | bytes accessed | tf_op | source)
XLA Modules:
  0.0 746.3 jit_solution(15933429299254345485)
XLA Ops:
  7.2 47.2 %all_gather.9 = bf16[512,512]{1,0:T(8,128)(2,1)S(1)} all-gather(bf16[32,512]{1,0:T(8,128)(2,1)} %param.8), channel_id=1, replica_groups=mesh['row'=16,'col'=16] {'col'}, dimensions={0}, use_global_device_ids=true | all-gather | bytes 557056 | tf_op jit(solution)/shard_map/all_gather | solution.py:37
  54.4 0.8 fusion.6
  55.2 0.1 copy.46
  55.3 2.8 copy.47
  58.2 0.1 copy.43
  58.3 4.4 copy.44
  62.6 0.5 mul.97
  63.2 3.1 convolution_bitcast_fusion.1
  66.3 0.5 mul.93
  66.9 1.2 copy-done.4
  68.1 3.1 convolution_bitcast_fusion.2
  71.2 0.0 reduce-scatter.10.cloned.1.call-start
  71.2 0.6 copy-done.11
  71.9 0.1 copy.49
  72.0 38.3 %all_gather.10 = bf16[512,512]{1,0:T(8,128)(2,1)S(1)} all-gather(bf16[32,512]{1,0:T(8,128)(2,1)S(1)} %copy-done.9), channel_id=1, replica_groups=mesh['row'=16,'col'=16] {'col'}, dimensions={0}, use_global_device_ids=true | all-gather | bytes 557056 | tf_op jit(solution)/shard_map/all_gather | solution.py:38
  110.3 0.5 mul.101
  110.8 4.5 convolution_bitcast_fusion
  115.4 5.2 copy.59
  120.6 86.1 %all-reduce.3.cloned.1.call-done = (f32[512,1792]{1,0:T(8,128)}, f32[512,1792]{1,0:T(8,128)}) async-done(((f32[512,1792]{1,0:T(8,128)}, f32[512,1792]{1,0:T(8,128)}), (f32[512,1792]{1,0:T(8,128)}, f32[512,1792]{1,0:T(8,128)})) %all-reduce.3.cloned.1.call-update) | async-done | bytes 7340048 | tf_op jit(solution)/shard_map/psum | solution.py:43
  206.7 71.8 %reduce-scatter.10.cloned.1.call-done = f32[32,1792]{1,0:T(8,128)} async-done(((f32[512,1792]{1,0:T(8,128)}), f32[32,1792]{1,0:T(8,128)}) %reduce-scatter.10.cloned.1.call-update) | async-done | bytes 229392 | tf_op jit(solution)/shard_map/reduce_scatter | solution.py:56
  278.5 1.9 multiply_convert_fusion.1
  280.4 1.4 stack.2
  281.8 8.8 %all-to-all-start = ((bf16[16,32,1792]{2,1,0:T(8,128)(2,1)}), bf16[16,32,1792]{2,1,0:T(8,128)(2,1)}, u32[]{:S(2)}, u32[]{:S(2)}) async-start(bf16[16,32,1792]{2,1,0:T(8,128)(2,1)} %stack.2), calls=%async_computation.1 | async-start | bytes 3670016 | tf_op jit(solution)/shard_map/all_to_all | solution.py:65
  290.7 4.3 multiply_convert_fusion
  295.0 1.3 copy-done.5
  296.2 2.2 fusion.4
  298.4 0.2 reduce-scatter.8.cloned.1.call-start
  298.7 17.1 %all-to-all-done = bf16[16,32,1792]{2,1,0:T(8,128)(2,1)} async-done(((bf16[16,32,1792]{2,1,0:T(8,128)(2,1)}), bf16[16,32,1792]{2,1,0:T(8,128)(2,1)}, u32[]{:S(2)}, u32[]{:S(2)}) %all-to-all-start) | async-done | bytes 1835040 | tf_op jit(solution)/shard_map/all_to_all | solution.py:65
  315.8 4.9 fusion.3
  320.6 9.8 %all-gather.2.cloned.1.call-done = bf16[512,1792]{1,0:T(8,128)(2,1)} async-done(((bf16[32,1792]{1,0:T(8,128)(2,1)}), bf16[512,1792]{1,0:T(8,128)(2,1)}) %all-gather.2.cloned.1.call-update) | async-done | bytes 1835024 | tf_op jit(solution)/shard_map/all_gather | solution.py:67
  330.4 4.4 convolution_add_fusion
  334.9 0.1 copy.52
  335.0 0.1 copy.53
  335.1 0.1 copy.54
  335.2 0.5 mul.117
  335.7 1.0 copy-done.6
  336.7 2.4 fusion
  339.0 0.5 mul.111
  339.6 2.6 fusion.2
  342.2 2.4 copy.55
  344.6 191.1 %reduce-scatter.6.cloned.1.call-done = f32[32,512]{1,0:T(8,128)} async-done(((f32[512,512]{1,0:T(8,128)}), f32[32,512]{1,0:T(8,128)}) %reduce-scatter.6.cloned.1.call-update) | async-done | bytes 65552 | tf_op jit(solution)/shard_map/reduce_scatter | solution.py:49
  535.7 1.5 convert_element_type.46
  537.2 0.5 mul.114
  537.7 1.0 copy-done.8
  538.7 1.2 fusion.1
  539.8 2.4 copy.56
  542.2 196.0 %reduce-scatter.8.cloned.1.call-done = f32[32,512]{1,0:T(8,128)} async-done(((f32[512,512]{1,0:T(8,128)}), f32[32,512]{1,0:T(8,128)}) %reduce-scatter.8.cloned.1.call-update) | async-done | bytes 65552 | tf_op jit(solution)/shard_map/reduce_scatter | solution.py:72
  738.3 1.5 convert_element_type.49
  (29 shorter events, 0.2 us)
Async XLA Ops:
  7.2 199.5 %all-reduce.3.cloned.1.call-start = ((), (), s32[]{:S(2)}) async-start(), calls=%async_computation.8 | async-start | bytes 14680064 | tf_op jit(solution)/shard_map/psum | solution.py:43
  55.3 2.8 copy-start.10
  58.1 5.0 copy-start
  63.2 3.1 copy-start.2
  66.3 1.8 copy-start.3
  66.8 1.2 copy-start.4
  71.2 0.7 copy-start.11
  71.2 0.8 copy-start.9
  71.2 207.3 %reduce-scatter.10.cloned.1.call-start = ((), (), s32[]{:S(2)}) async-start(), calls=%async_computation.7 | async-start | bytes 3899392 | tf_op jit(solution)/shard_map/reduce_scatter | solution.py:56
  120.6 209.8 %all-gather.2.cloned.1.call-start = ((), (), s32[]{:S(2)}) async-start(), calls=%async_computation.5 | async-start | bytes 1949696 | tf_op jit(solution)/shard_map/all_gather | solution.py:67
  281.8 33.9 %all-to-all-start = ((bf16[16,32,1792]{2,1,0:T(8,128)(2,1)}), bf16[16,32,1792]{2,1,0:T(8,128)(2,1)}, u32[]{:S(2)}, u32[]{:S(2)}) async-start(bf16[16,32,1792]{2,1,0:T(8,128)(2,1)} %stack.2), calls=%async_computation.1 | async-start | bytes 3670016 | tf_op jit(solution)/shard_map/all_to_all | solution.py:65
  290.6 245.1 %reduce-scatter.6.cloned.1.call-start = ((), (), s32[]{:S(2)}) async-start(), calls=%async_computation.4 | async-start | bytes 1114112 | tf_op jit(solution)/shard_map/reduce_scatter | solution.py:49
  290.6 5.6 copy-start.7
  295.0 1.3 copy-start.5
  298.4 439.8 %reduce-scatter.8.cloned.1.call-start = ((), (), s32[]{:S(2)}) async-start(), calls=%async_computation.6 | async-start | bytes 1114112 | tf_op jit(solution)/shard_map/reduce_scatter | solution.py:72
  315.7 14.7 %copy-start.1 = (bf16[512,1792]{0,1:T(8,128)(2,1)S(1)}, bf16[512,1792]{0,1:T(8,128)(2,1)}, u32[]{:S(2)}) copy-start(bf16[512,1792]{0,1:T(8,128)(2,1)} %copy-done) | copy-start | bytes 5505028
  335.2 1.5 copy-start.6
  537.2 1.5 copy-start.8
Sparse Core Ops, SparseCore 0:
  71.3 135.3 all-reduce.2
  209.3 69.1 reduce-scatter.9
  280.5 49.8 all-gather.1
  334.1 201.5 reduce-scatter.5
  539.4 198.8 reduce-scatter.7
